TPU v7x, 32 devices: a whole 2x2x4 slice. The times are simulated.
32 devices in a mesh: seq: 8 (over z, x), wa: 4 (over y, core).
Axes of the slice: x: 2, y: 2, z: 4, core: 2. Of those that a mesh axis runs over, the one named last changes fastest.
Arguments:
- tokens: bfloat16 [2048, 1024], P('seq'), may hold values from -6 to 6
- gain_mix: float32 [1024], replicated, may hold values from 0.5 to 1.5
- w_z: bfloat16 [1024, 1536], P('seq', 'wa'), may hold values from -0.1875 to 0.1875
- w_x: bfloat16 [1024, 1536], P('seq', 'wa'), may hold values from -0.1875 to 0.1875
- w_bc: bfloat16 [1024, 256], P('seq'), may hold values from -0.046875 to 0.046875
- w_dt: bfloat16 [1024, 24], P('seq', 'wa'), may hold values from -0.1875 to 0.1875
- conv_x: float32 [4, 1536], P(None, 'wa'), may hold values from -3 to 3
- conv_bc: float32 [4, 256], replicated, may hold values from -3 to 3
- dt_bias: float32 [24], P('wa'), may hold values from -1 to 1
- a_log: float32 [24], P('wa'), may hold values from -10.5 to -3
- d_skip: float32 [24], P('wa'), may hold values from 0.5 to 1.5
- w_out: bfloat16 [1536, 1024], P('wa', 'seq'), may hold values from -0.0390625 to 0.0390625
- w_q: bfloat16 [1024, 512], P('seq', 'wa'), may hold values from -0.1875 to 0.1875
- w_kv: bfloat16 [1024, 256], P('seq'), may hold values from -0.1875 to 0.1875
- w_o: bfloat16 [512, 1024], P('wa', 'seq'), may hold values from -1 to 1
- gain_ffn: float32 [1024], replicated, may hold values from 0.5 to 1.5
- w_gate: bfloat16 [1024, 2048], P('seq', 'wa'), may hold values from -0.1875 to 0.1875
- w_up: bfloat16 [1024, 2048], P('seq', 'wa'), may hold values from -0.1875 to 0.1875
- w_down: bfloat16 [2048, 1024], P('wa', 'seq'), may hold values from -0.125 to 0.125
- cotangent: bfloat16 [2048, 1024], P('seq'), may hold values from -6 to 6
Outputs:
- output: bfloat16 [2048, 1024], P('seq', 'wa')
- grad_tokens: float32 [2048, 1024], P('seq')
- grad_gain_mix: float32 [1024], replicated
- grad_w_z: float32 [1024, 1536], P('seq', 'wa')
- grad_w_x: float32 [1024, 1536], P('seq', 'wa')
- grad_w_bc: float32 [1024, 256], P('seq')
- grad_w_dt: float32 [1024, 24], P('seq', 'wa')
- grad_conv_x: float32 [4, 1536], P(None, 'wa')
- grad_conv_bc: float32 [4, 256], replicated
- grad_dt_bias: float32 [24], P('wa')
- grad_a_log: float32 [24], P('wa')
- grad_d_skip: float32 [24], P('wa')
- grad_w_out: float32 [1536, 1024], P('wa', 'seq')
- grad_w_q: float32 [1024, 512], P('seq', 'wa')
- grad_w_kv: float32 [1024, 256], P('seq')
- grad_w_o: float32 [512, 1024], P('wa', 'seq')
- grad_gain_ffn: float32 [1024], replicated
- grad_w_gate: float32 [1024, 2048], P('seq', 'wa')
- grad_w_up: float32 [1024, 2048], P('seq', 'wa')
- grad_w_down: float32 [2048, 1024], P('wa', 'seq')
All inputs are finite; a program needn't handle non-finite values.
Results may differ from a plain program's by a relative error of at most 0.012.
Values may be sent and summed in bfloat16 or wider, within the bound.
A program may use at most 128 MiB of HBM per device.

v0:
```python
import jax
import jax.numpy as jnp
from jax import lax
from jax.sharding import PartitionSpec as P

NS = 128
CONVK = 4
QH = 8
KVH = 2
HD = 64


EPS = 1e-05
ROPE_BASE = 100000000000.0
highest = lax.Precision.HIGHEST


def passed_along(value, axis, steps):
    count = lax.axis_size(axis)
    leading, last = (max(0, -steps), min(count, count - steps))
    return lax.ppermute(value, axis, [(source, source + steps) for source in range(leading, last)])


def prefix(x, axis, combine, identity, reverse):
    length, mine = (lax.axis_size(axis), lax.axis_index(axis))
    everything = jax.tree.map(lambda part: lax.all_gather(part, axis), x)
    start = jax.tree.map(
        lambda part, zero: jnp.broadcast_to(jnp.asarray(zero, part.dtype), part.shape), x, identity
    )

    def step(k, before):
        at = length - 1 - k if reverse else k
        reached = at > mine if reverse else at < mine
        new = combine(before, jax.tree.map(lambda part: part[at], everything))
        return jax.tree.map(lambda a, b: jnp.where(reached, a, b), new, before)

    return lax.fori_loop(0, length, step, start)


def project(left_side, right_side):
    return jnp.dot(left_side, right_side, preferred_element_type=jnp.float32)


def rms_scale(row_values):
    return lax.rsqrt(jnp.mean(row_values * row_values, axis=-1, keepdims=True) + EPS)


def rope_tables(positions):
    frequency = ROPE_BASE ** (-(jnp.arange(HD // 2, dtype=jnp.float32) * 2.0 / HD))
    angles = positions.astype(jnp.float32)[:, None] * frequency[None, :]
    return (jnp.cos(angles), jnp.sin(angles))


def rotate(values, cosine, sine):
    half_width = values.shape[-1] // 2
    first_half = values[..., :half_width]
    second_half = values[..., half_width:]
    cos_part = cosine[:, None, :]
    sin_part = sine[:, None, :]
    return jnp.concatenate(
        [
            first_half * cos_part - second_half * sin_part,
            second_half * cos_part + first_half * sin_part,
        ],
        axis=-1,
    )


def unrotate(gradients, cosine, sine):
    half_width = gradients.shape[-1] // 2
    first_half = gradients[..., :half_width]
    second_half = gradients[..., half_width:]
    cos_part = cosine[:, None, :]
    sin_part = sine[:, None, :]
    return jnp.concatenate(
        [
            first_half * cos_part + second_half * sin_part,
            second_half * cos_part - first_half * sin_part,
        ],
        axis=-1,
    )


def conv_silu(pre_values, kernel, edge_rows):
    length = pre_values.shape[0]
    padded = jnp.concatenate([edge_rows, pre_values], axis=0)
    running = kernel[0] * padded[0:length]
    for offset in range(1, CONVK):
        running = running + kernel[offset] * padded[offset : offset + length]
    return jax.nn.silu(running)


def prepare(x_input, bc_input, dt_input, edge_x, edge_bc, conv_x, conv_bc, dt_bias, a_log):
    length = x_input.shape[0]
    head_count = a_log.shape[0]
    x_conv = conv_silu(x_input, conv_x, edge_x).reshape(length, head_count, -1)
    bc_conv = conv_silu(bc_input, conv_bc, edge_bc)
    step_size = jax.nn.softplus(dt_input + dt_bias[None, :])
    log_decay = -jnp.exp(a_log)[None, :] * step_size
    return (x_conv, bc_conv[:, :NS], bc_conv[:, NS:], step_size, log_decay)


def ssd_state(x_conv, b_mat, step_size, log_decay):
    cumulative = jnp.cumsum(log_decay, axis=0)
    tail_weight = jnp.exp(cumulative[-1][None, :] - cumulative) * step_size
    local_state = jnp.einsum("sh,shp,sn->hpn", tail_weight, x_conv, b_mat, precision=highest)
    return (jnp.exp(cumulative[-1]), local_state)


def ssd_output(x_conv, b_mat, c_mat, step_size, log_decay, start_state):
    cumulative = jnp.cumsum(log_decay, axis=0)
    length = x_conv.shape[0]
    causal = (
        jnp.arange(length, dtype=jnp.int32)[:, None] >= jnp.arange(length, dtype=jnp.int32)[None, :]
    )
    gap_sums = cumulative[:, None, :] - cumulative[None, :, :]
    decays = jnp.exp(jnp.where(causal[:, :, None], gap_sums, -1e30))
    intersections = jnp.dot(c_mat, b_mat.T, precision=highest)
    mixing = decays * intersections[:, :, None] * step_size[None, :, :]
    inner_part = jnp.einsum("tsh,shp->thp", mixing, x_conv, precision=highest)
    carried = (
        jnp.einsum("tn,hpn->thp", c_mat, start_state, precision=highest)
        * jnp.exp(cumulative)[:, :, None]
    )
    return inner_part + carried


def state_part(x_input, bc_input, dt_input, edge_x, edge_bc, conv_x, conv_bc, dt_bias, a_log):
    x_conv, b_mat, c_mat, step_size, log_decay = prepare(
        x_input, bc_input, dt_input, edge_x, edge_bc, conv_x, conv_bc, dt_bias, a_log
    )
    return ssd_state(x_conv, b_mat, step_size, log_decay)


def output_part(
    z_input,
    x_input,
    bc_input,
    dt_input,
    edge_x,
    edge_bc,
    conv_x,
    conv_bc,
    dt_bias,
    a_log,
    d_skip,
    start_state,
):
    x_conv, b_mat, c_mat, step_size, log_decay = prepare(
        x_input, bc_input, dt_input, edge_x, edge_bc, conv_x, conv_bc, dt_bias, a_log
    )
    ssm_out = (
        ssd_output(x_conv, b_mat, c_mat, step_size, log_decay, start_state)
        + d_skip[None, :, None] * x_conv
    )
    return ssm_out.reshape(ssm_out.shape[0], -1) * jax.nn.silu(z_input)


def chain_link(earlier, later):
    return (earlier[0] * later[0], later[0][:, None, None] * earlier[1] + later[1])


def block_of():
    return 512


def score_parts(
    queries, query_pos, key_rows, key_pos, value_rows, d_attn_rows, sums_rows, delta_rows
):
    scores = jnp.einsum(
        "tgd,nd->gtn", queries, key_rows, preferred_element_type=jnp.float32
    ) * HD ** (-0.5)
    allowed = key_pos[None, None, :] <= query_pos[None, :, None]
    probability = jnp.where(allowed, jnp.exp(scores - sums_rows[:, :, None]), 0.0)
    d_probs = jnp.einsum("tgd,nd->gtn", d_attn_rows, value_rows, preferred_element_type=jnp.float32)
    d_scores = (probability * (d_probs - delta_rows[:, :, None])).astype(jnp.bfloat16)
    return (probability, d_scores)


def key_value_grads(
    queries, query_pos, key_rows, key_pos, value_rows, d_attn_rows, sums_rows, delta_rows
):
    probability, d_scores = score_parts(
        queries, query_pos, key_rows, key_pos, value_rows, d_attn_rows, sums_rows, delta_rows
    )
    d_key = jnp.einsum(
        "gtn,tgd->nd", d_scores, queries, preferred_element_type=jnp.float32
    ) * HD ** (-0.5)
    d_value = jnp.einsum(
        "gtn,tgd->nd",
        probability.astype(jnp.bfloat16),
        d_attn_rows,
        preferred_element_type=jnp.float32,
    )
    return jnp.concatenate([d_key, d_value], axis=1)


def attend(queries, query_pos, key_all, value_all, key_limit):
    block_size = block_of()
    group_count = queries.shape[1]
    length = queries.shape[0]
    block_count = (key_limit + block_size - 1) // block_size

    def attend_visit_block(index, state_carry):
        run_max, run_sum, weighted_sum = state_carry
        offset = index * block_size
        key_rows = lax.dynamic_slice_in_dim(key_all, offset, block_size, 0)
        value_rows = lax.dynamic_slice_in_dim(value_all, offset, block_size, 0)
        key_pos = offset + jnp.arange(block_size, dtype=jnp.int32)
        scores = jnp.einsum(
            "tgd,nd->gtn", queries, key_rows, preferred_element_type=jnp.float32
        ) * HD ** (-0.5)
        allowed = key_pos[None, None, :] <= query_pos[None, :, None]
        new_max = jnp.maximum(run_max, jnp.max(jnp.where(allowed, scores, -1e30), axis=-1))
        weights = jnp.where(allowed, jnp.exp(scores - new_max[:, :, None]), 0.0)
        rescale = jnp.exp(run_max - new_max)
        run_sum = run_sum * rescale + jnp.sum(weights, axis=-1)
        weighted_sum = weighted_sum * rescale[:, :, None] + jnp.einsum(
            "gtn,nd->gtd",
            weights.astype(jnp.bfloat16),
            value_rows,
            preferred_element_type=jnp.float32,
        )
        return (new_max, run_sum, weighted_sum)

    initial = (
        jnp.full((group_count, length), -1e30, jnp.float32),
        jnp.zeros((group_count, length), jnp.float32),
        jnp.zeros((group_count, length, HD), jnp.float32),
    )
    run_max, run_sum, weighted_sum = lax.fori_loop(0, block_count, attend_visit_block, initial)
    attn_heads = (weighted_sum / run_sum[:, :, None]).transpose(1, 0, 2).astype(jnp.bfloat16)
    return (attn_heads, run_max + jnp.log(run_sum))


def query_grad(
    queries, query_pos, key_all, value_all, d_attn_heads, log_sums, out_delta, key_limit
):
    block_size = block_of()
    block_count = (key_limit + block_size - 1) // block_size

    def query_visit_block(index, running):
        offset = index * block_size
        key_rows = lax.dynamic_slice_in_dim(key_all, offset, block_size, 0)
        value_rows = lax.dynamic_slice_in_dim(value_all, offset, block_size, 0)
        key_pos = offset + jnp.arange(block_size, dtype=jnp.int32)
        probability, d_scores = score_parts(
            queries, query_pos, key_rows, key_pos, value_rows, d_attn_heads, log_sums, out_delta
        )
        step_grad = jnp.einsum(
            "gtn,nd->tgd", d_scores, key_rows, preferred_element_type=jnp.float32
        ) * HD ** (-0.5)
        return running + step_grad

    return lax.fori_loop(0, block_count, query_visit_block, jnp.zeros(queries.shape, jnp.float32))


def spread_rows(values, seq_count):
    return jnp.broadcast_to(values[None], (seq_count,) + values.shape)


def per_device(
    tokens,
    gain_mix,
    w_z,
    w_x,
    w_bc,
    w_dt,
    conv_x,
    conv_bc,
    dt_bias,
    a_log,
    d_skip,
    w_out,
    w_q,
    w_kv,
    w_o,
    gain_ffn,
    w_gate,
    w_up,
    w_down,
    cotangent,
):
    local_rows = tokens.shape[0]
    seq_count = lax.axis_size("seq")
    seq_index = lax.axis_index("seq")
    wa_index = lax.axis_index("wa")
    key_limit = (seq_index + 1) * local_rows
    tokens_wide = tokens.astype(jnp.float32)
    scale_mix = rms_scale(tokens_wide)
    normed = (tokens_wide * scale_mix * gain_mix).astype(jnp.bfloat16)
    gathered = (
        lax.all_gather(w_z, "seq", axis=0, tiled=True),
        lax.all_gather(w_x, "seq", axis=0, tiled=True),
        lax.all_gather(w_bc, "seq", axis=0, tiled=True),
        lax.all_gather(w_dt, "seq", axis=0, tiled=True),
        lax.all_gather(w_out, "seq", axis=1, tiled=True),
        lax.all_gather(w_q, "seq", axis=0, tiled=True),
        lax.all_gather(w_kv, "seq", axis=0, tiled=True),
        lax.all_gather(w_o, "seq", axis=1, tiled=True),
        lax.all_gather(w_gate, "seq", axis=0, tiled=True),
        lax.all_gather(w_up, "seq", axis=0, tiled=True),
        lax.all_gather(w_down, "seq", axis=1, tiled=True),
    )
    (
        full_z,
        full_x,
        full_bc,
        full_dt,
        full_out,
        full_q,
        full_kv,
        full_o,
        full_gate,
        full_up,
        full_down,
    ) = gathered
    z_proj = project(normed, full_z)
    x_proj = project(normed, full_x)
    bc_proj = project(normed, full_bc)
    dt_proj = project(normed, full_dt)
    edge_count = CONVK - 1
    width_x = x_proj.shape[1]
    edge_send = jnp.concatenate(
        [x_proj[local_rows - edge_count :], bc_proj[local_rows - edge_count :]], axis=1
    )
    edge_recv = passed_along(edge_send, "seq", 1)
    mixer_inputs = (
        x_proj,
        bc_proj,
        dt_proj,
        edge_recv[:, :width_x],
        edge_recv[:, width_x:],
        conv_x,
        conv_bc,
        dt_bias,
        a_log,
    )
    decay_total, local_state = state_part(*mixer_inputs)
    identity = (jnp.ones_like(decay_total), jnp.zeros_like(local_state))
    start_state = prefix((decay_total, local_state), "seq", chain_link, identity, False)[1]
    ssm_gated, pull_output = jax.vjp(output_part, z_proj, *mixer_inputs, d_skip, start_state)
    gated = ssm_gated.astype(jnp.bfloat16)
    local_query = full_q.shape[1] // HD
    kv_head = wa_index * local_query // (QH // KVH)
    positions = seq_index * local_rows + jnp.arange(local_rows, dtype=jnp.int32)
    cosine, sine = rope_tables(positions)
    q_proj = project(normed, full_q).reshape(local_rows, local_query, HD)
    kv_proj = project(normed, full_kv)
    k_proj = lax.dynamic_slice_in_dim(kv_proj, kv_head * HD, HD, 1)
    v_proj = lax.dynamic_slice_in_dim(kv_proj, KVH * HD + kv_head * HD, HD, 1)
    q_rot = rotate(q_proj, cosine, sine).astype(jnp.bfloat16)
    k_rot = rotate(k_proj[:, None, :], cosine, sine)[:, 0, :].astype(jnp.bfloat16)
    v_val = v_proj.astype(jnp.bfloat16)
    key_all, value_all = (
        lax.all_gather(k_rot, "seq", axis=0, tiled=True),
        lax.all_gather(v_val, "seq", axis=0, tiled=True),
    )
    attn_heads, log_sums = attend(q_rot, positions, key_all, value_all, key_limit)
    attn_out = attn_heads.reshape(local_rows, local_query * HD)
    mixer_total = lax.psum(project(gated, full_out) + project(attn_out, full_o), "wa")
    hidden = tokens_wide + mixer_total
    scale_ffn = rms_scale(hidden)
    hnormed = (hidden * scale_ffn * gain_ffn).astype(jnp.bfloat16)
    gate_proj = project(hnormed, full_gate)
    up_proj = project(hnormed, full_up)
    activated = (jax.nn.silu(gate_proj) * up_proj).astype(jnp.bfloat16)
    ffn_own = lax.psum_scatter(project(activated, full_down), "wa", scatter_dimension=1, tiled=True)
    own_width = ffn_own.shape[1]
    hidden_own = lax.dynamic_slice_in_dim(hidden, wa_index * own_width, own_width, 1)
    output = (hidden_own + ffn_own).astype(jnp.bfloat16)
    cot_wide = cotangent.astype(jnp.float32)
    d_act = project(cotangent, full_down.T)
    sigmoid_gate = jax.nn.sigmoid(gate_proj)
    d_gate = (d_act * up_proj * sigmoid_gate * (1.0 + gate_proj * (1.0 - sigmoid_gate))).astype(
        jnp.bfloat16
    )
    d_up = (d_act * gate_proj * sigmoid_gate).astype(jnp.bfloat16)
    d_hnormed = lax.psum(project(d_gate, full_gate.T) + project(d_up, full_up.T), "wa")
    hidden_hat = hidden * scale_ffn
    weighted_ffn = d_hnormed * gain_ffn
    d_hidden = cot_wide + scale_ffn * (
        weighted_ffn - hidden_hat * jnp.mean(weighted_ffn * hidden_hat, axis=-1, keepdims=True)
    )
    grad_gain_ffn = jnp.sum(d_hnormed * hidden_hat, axis=0)
    d_hidden_b = d_hidden.astype(jnp.bfloat16)
    part_w_out = project(gated.T, d_hidden_b)
    part_w_o = project(attn_out.T, d_hidden_b)
    part_w_gate = project(hnormed.T, d_gate)
    part_w_up = project(hnormed.T, d_up)
    part_w_down = project(activated.T, cotangent)
    d_gated = project(d_hidden_b, full_out.T)
    d_attn = project(d_hidden_b, full_o.T).astype(jnp.bfloat16)
    d_attn_heads = d_attn.reshape(local_rows, local_query, HD)
    out_delta = jnp.sum(
        d_attn_heads.astype(jnp.float32) * attn_heads.astype(jnp.float32), axis=-1
    ).T
    d_q_rot = query_grad(
        q_rot, positions, key_all, value_all, d_attn_heads, log_sums, out_delta, key_limit
    )
    last_query = key_limit - 1
    block_size = block_of()

    def one_block(offset):
        first_key = offset

        def compute_block(first_key):
            key_rows = lax.dynamic_slice_in_dim(key_all, first_key, block_size, 0)
            value_rows = lax.dynamic_slice_in_dim(value_all, first_key, block_size, 0)
            key_pos = first_key + jnp.arange(block_size, dtype=jnp.int32)
            return key_value_grads(
                q_rot, positions, key_rows, key_pos, value_rows, d_attn_heads, log_sums, out_delta
            )

        def empty_block(first_key):
            return jnp.zeros((block_size, 2 * HD), jnp.float32)

        return lax.cond(first_key <= last_query, compute_block, empty_block, first_key)

    pieces = lax.map(
        one_block,
        jnp.arange(local_rows * lax.axis_size("seq") // block_size, dtype=jnp.int32) * block_size,
    )
    key_grad = lax.psum_scatter(
        pieces.reshape(local_rows * lax.axis_size("seq"), 2 * HD),
        "seq",
        scatter_dimension=0,
        tiled=True,
    )
    d_key_own = unrotate(key_grad[:, None, :HD], cosine, sine)[:, 0, :]
    d_value_own = key_grad[:, HD:]
    head_pick = (jnp.arange(KVH, dtype=jnp.int32) == kv_head).astype(jnp.float32)
    d_kv_part = jnp.concatenate(
        [
            (head_pick[None, :, None] * d_key_own[:, None, :]).reshape(local_rows, KVH * HD),
            (head_pick[None, :, None] * d_value_own[:, None, :]).reshape(local_rows, KVH * HD),
        ],
        axis=1,
    )
    d_q = unrotate(d_q_rot, cosine, sine).reshape(local_rows, -1).astype(jnp.bfloat16)
    out_grads = pull_output(d_gated)
    direct = out_grads[11]
    d_end = prefix((decay_total, direct), "seq", chain_link, identity, True)[1]
    d_decay = jnp.sum(d_end * start_state, axis=(1, 2))
    _, pull_state = jax.vjp(state_part, *mixer_inputs)
    state_grads = pull_state((d_decay, d_end))
    merged = tuple(map(jnp.add, out_grads[1:10], state_grads))
    (
        d_x_in,
        d_bc_in,
        d_dt_in,
        d_edge_x,
        d_edge_bc,
        grad_conv_x,
        d_conv_bc_part,
        grad_dt_bias,
        grad_a_log,
    ) = merged
    edge_back = passed_along(jnp.concatenate([d_edge_x, d_edge_bc], axis=1), "seq", -1)
    d_x_in = jnp.concatenate(
        [
            d_x_in[: local_rows - edge_count],
            d_x_in[local_rows - edge_count :] + edge_back[:, :width_x],
        ],
        axis=0,
    )
    d_bc_in = jnp.concatenate(
        [
            d_bc_in[: local_rows - edge_count],
            d_bc_in[local_rows - edge_count :] + edge_back[:, width_x:],
        ],
        axis=0,
    )
    d_z_b = out_grads[0].astype(jnp.bfloat16)
    d_x_b = d_x_in.astype(jnp.bfloat16)
    d_dt_b = d_dt_in.astype(jnp.bfloat16)
    d_normed_part = (
        project(d_z_b, full_z.T)
        + project(d_x_b, full_x.T)
        + project(d_dt_b, full_dt.T)
        + project(d_q, full_q.T)
    )
    d_normed_sum, d_bc_full, d_kv_full, grad_conv_bc = lax.psum(
        (d_normed_part, d_bc_in, d_kv_part, d_conv_bc_part), "wa"
    )
    d_bc_b = d_bc_full.astype(jnp.bfloat16)
    d_kv_b = d_kv_full.astype(jnp.bfloat16)
    d_normed = d_normed_sum + project(d_bc_b, full_bc.T) + project(d_kv_b, full_kv.T)
    tokens_hat = tokens_wide * scale_mix
    weighted_mix = d_normed * gain_mix
    grad_tokens = d_hidden + scale_mix * (
        weighted_mix - tokens_hat * jnp.mean(weighted_mix * tokens_hat, axis=-1, keepdims=True)
    )
    grad_gain_mix = jnp.sum(d_normed * tokens_hat, axis=0)
    part_w_z = project(normed.T, d_z_b)
    part_w_x = project(normed.T, d_x_b)
    part_w_bc = project(normed.T, d_bc_b)
    part_w_dt = project(normed.T, d_dt_b)
    part_w_q = project(normed.T, d_q)
    part_w_kv = project(normed.T, d_kv_b)
    summed = (
        lax.psum_scatter(part_w_z, "seq", scatter_dimension=0, tiled=True),
        lax.psum_scatter(part_w_x, "seq", scatter_dimension=0, tiled=True),
        lax.psum_scatter(part_w_bc, "seq", scatter_dimension=0, tiled=True),
        lax.psum_scatter(part_w_dt, "seq", scatter_dimension=0, tiled=True),
        lax.psum_scatter(part_w_out, "seq", scatter_dimension=1, tiled=True),
        lax.psum_scatter(part_w_q, "seq", scatter_dimension=0, tiled=True),
        lax.psum_scatter(part_w_kv, "seq", scatter_dimension=0, tiled=True),
        lax.psum_scatter(part_w_o, "seq", scatter_dimension=1, tiled=True),
        lax.psum_scatter(part_w_gate, "seq", scatter_dimension=0, tiled=True),
        lax.psum_scatter(part_w_up, "seq", scatter_dimension=0, tiled=True),
        lax.psum_scatter(part_w_down, "seq", scatter_dimension=1, tiled=True),
        lax.psum_scatter(
            spread_rows(grad_gain_mix, seq_count), "seq", scatter_dimension=0, tiled=True
        ),
        lax.psum_scatter(
            spread_rows(grad_gain_ffn, seq_count), "seq", scatter_dimension=0, tiled=True
        ),
        lax.psum_scatter(
            spread_rows(grad_conv_x, seq_count), "seq", scatter_dimension=0, tiled=True
        ),
        lax.psum_scatter(
            spread_rows(grad_conv_bc, seq_count), "seq", scatter_dimension=0, tiled=True
        ),
        lax.psum_scatter(
            spread_rows(grad_dt_bias, seq_count), "seq", scatter_dimension=0, tiled=True
        ),
        lax.psum_scatter(
            spread_rows(grad_a_log, seq_count), "seq", scatter_dimension=0, tiled=True
        ),
        lax.psum_scatter(
            spread_rows(out_grads[10], seq_count), "seq", scatter_dimension=0, tiled=True
        ),
    )
    (
        grad_w_z,
        grad_w_x,
        grad_w_bc,
        grad_w_dt,
        grad_w_out,
        grad_w_q,
        grad_w_kv,
        grad_w_o,
        grad_w_gate,
        grad_w_up,
        grad_w_down,
        sum_gain_mix,
        sum_gain_ffn,
        sum_conv_x,
        sum_conv_bc,
        sum_dt_bias,
        sum_a_log,
        sum_d_skip,
    ) = summed
    return (
        output,
        grad_tokens,
        sum_gain_mix[0],
        grad_w_z,
        grad_w_x,
        grad_w_bc,
        grad_w_dt,
        sum_conv_x[0],
        sum_conv_bc[0],
        sum_dt_bias[0],
        sum_a_log[0],
        sum_d_skip[0],
        grad_w_out,
        grad_w_q,
        grad_w_kv,
        grad_w_o,
        sum_gain_ffn[0],
        grad_w_gate,
        grad_w_up,
        grad_w_down,
    )


def solution(mesh):
    placed = (
        P("seq", None),
        P(),
        P("seq", "wa"),
        P("seq", "wa"),
        P("seq", None),
        P("seq", "wa"),
        P(None, "wa"),
        P(),
        P("wa"),
        P("wa"),
        P("wa"),
        P("wa", "seq"),
        P("seq", "wa"),
        P("seq", None),
        P("wa", "seq"),
        P(),
        P("seq", "wa"),
        P("seq", "wa"),
        P("wa", "seq"),
        P("seq", None),
    )
    return jax.shard_map(
        per_device,
        mesh=mesh,
        in_specs=placed,
        out_specs=(
            P("seq", "wa"),
            P("seq", None),
            P(),
            P("seq", "wa"),
            P("seq", "wa"),
            P("seq", None),
            P("seq", "wa"),
            P(None, "wa"),
            P(),
            P("wa"),
            P("wa"),
            P("wa"),
            P("wa", "seq"),
            P("seq", "wa"),
            P("seq", None),
            P("wa", "seq"),
            P(),
            P("seq", "wa"),
            P("seq", "wa"),
            P("wa", "seq"),
        ),
        check_vma=False,
    )
```

profile of v0, /device:TPU:0, one launch (start us, length us, event | category | flops | bytes accessed | tf_op | source)
XLA Modules:
  0.0 1618.0 jit_solution(1162399048877367529)
XLA Ops:
  8.5 33.5 %all_gather.58 = bf16[1024,256]{1,0:T(8,128)(2,1)S(1)} all-gather(bf16[128,256]{1,0:T(8,128)(2,1)} %param.37), channel_id=1, replica_groups=mesh['seq'=8,'wa'=4] {'seq'}, dimensions={0}, use_global_device_ids=true | all-gather | bytes 589824 | tf_op jit(solution)/shard_map/all_gather | solution.py:295
  43.7 32.0 %all_gather.57 = bf16[1024,384]{1,0:T(8,128)(2,1)S(1)} all-gather(bf16[128,384]{1,0:T(8,128)(2,1)S(1)} %copy-done.68), channel_id=1, replica_groups=mesh['seq'=8,'wa'=4] {'seq'}, dimensions={0}, use_global_device_ids=true | all-gather | bytes 884736 | tf_op jit(solution)/shard_map/all_gather | solution.py:294
  81.2 26.1 %all_gather.59 = bf16[1024,6]{0,1:T(8,128)(2,1)S(1)} all-gather(bf16[128,6]{0,1:T(8,128)(2,1)S(1)} %copy-done.129), channel_id=1, replica_groups=mesh['seq'=8,'wa'=4] {'seq'}, dimensions={0}, use_global_device_ids=true | all-gather | bytes 13824 | tf_op jit(solution)/shard_map/all_gather | solution.py:296
  110.1 30.9 %all_gather.67 = bf16[1024,128]{1,0:T(8,128)(2,1)S(1)} all-gather(bf16[128,128]{1,0:T(8,128)(2,1)S(1)} %copy-done.88), channel_id=1, replica_groups=mesh['seq'=8,'wa'=4] {'seq'}, dimensions={0}, use_global_device_ids=true | all-gather | bytes 294912 | tf_op jit(solution)/shard_map/all_gather | solution.py:298
  141.4 31.4 %all_gather.65 = bf16[1024,256]{1,0:T(8,128)(2,1)S(1)} all-gather(bf16[128,256]{1,0:T(8,128)(2,1)S(1)} %copy-done.78), channel_id=1, replica_groups=mesh['seq'=8,'wa'=4] {'seq'}, dimensions={0}, use_global_device_ids=true | all-gather | bytes 589824 | tf_op jit(solution)/shard_map/all_gather | solution.py:299
  174.7 30.7 %all_gather.68 = bf16[2048,64]{0,1:T(8,128)(2,1)S(1)} all-gather(bf16[256,64]{0,1:T(8,128)(2,1)S(1)} %dynamic-slice_convert_fusion), channel_id=1, replica_groups=mesh['seq'=8,'wa'=4] {'seq'}, dimensions={0}, use_global_device_ids=true | all-gather | bytes 294912 | tf_op jit(solution)/shard_map/all_gather | solution.py:357
  205.4 30.9 %all-gather.1 = bf16[2048,1,64]{0,2,1:T(8,128)(2,1)S(1)} all-gather(bf16[256,1,64]{0,2,1:T(8,128)(2,1)S(1)} %pad_maximum_fusion.9), channel_id=3, replica_groups=mesh['seq'=8,'wa'=4] {'seq'}, dimensions={0}, use_global_device_ids=true | all-gather | bytes 294912 | tf_op jit(solution)/shard_map/all_gather | solution.py:356
  244.7 19.9 %all-gather.3 = f32[8,1,6]{2,1,0:T(1,128)S(1)} all-gather(f32[1,1,6]{2,1,0:T(1,128)S(1)} %bitcast.495), channel_id=1, replica_groups=mesh['seq'=8,'wa'=4] {'seq'}, dimensions={0}, use_global_device_ids=true | all-gather | bytes 216 | tf_op jit(solution)/shard_map/all_gather | solution.py:26
  264.6 28.1 %all_gather.69 = bf16[128,1024]{1,0:T(8,128)(2,1)S(1)} all-gather(bf16[128,128]{1,0:T(8,128)(2,1)S(1)} %copy-done.89), channel_id=1, replica_groups=mesh['seq'=8,'wa'=4] {'seq'}, dimensions={1}, use_global_device_ids=true | all-gather | bytes 294912 | tf_op jit(solution)/shard_map/all_gather | solution.py:300
  293.1 33.7 %all_gather.63 = bf16[1024,384]{1,0:T(8,128)(2,1)} all-gather(bf16[128,384]{1,0:T(8,128)(2,1)S(1)} %copy-done.69), channel_id=1, replica_groups=mesh['seq'=8,'wa'=4] {'seq'}, dimensions={0}, use_global_device_ids=true | all-gather | bytes 884736 | tf_op jit(solution)/shard_map/all_gather | solution.py:293
  326.8 28.7 %all_gather.64 = bf16[384,1024]{1,0:T(8,128)(2,1)} all-gather(bf16[384,128]{1,0:T(8,128)(2,1)S(1)} %copy-done.70), channel_id=1, replica_groups=mesh['seq'=8,'wa'=4] {'seq'}, dimensions={1}, use_global_device_ids=true | all-gather | bytes 884736 | tf_op jit(solution)/shard_map/all_gather | solution.py:297
  375.8 32.2 %all-reduce.52.cloned.1.call-done = f32[256,1024]{1,0:T(8,128)} async-done(((f32[256,1024]{1,0:T(8,128)}), f32[256,1024]{1,0:T(8,128)}) %all-reduce.52.cloned.1.call-update) | async-done | bytes 1048592 | tf_op jit(solution)/shard_map/psum | solution.py:361
  409.6 41.3 %all-gather.12.cloned.1.call-done = bf16[1024,512]{1,0:T(8,128)(2,1)} async-done(((bf16[128,512]{1,0:T(8,128)(2,1)}), bf16[1024,512]{1,0:T(8,128)(2,1)}) %all-gather.12.cloned.1.call-update) | async-done | bytes 1048592 | tf_op jit(solution)/shard_map/all_gather | solution.py:302
  453.4 38.5 %all-gather.10.cloned.1.call-done = bf16[1024,512]{1,0:T(8,128)(2,1)} async-done(((bf16[128,512]{1,0:T(8,128)(2,1)}), bf16[1024,512]{1,0:T(8,128)(2,1)}) %all-gather.10.cloned.1.call-update) | async-done | bytes 1048592 | tf_op jit(solution)/shard_map/all_gather | solution.py:301
  494.3 37.6 %all-gather.14.cloned.1.call-done = bf16[512,1024]{1,0:T(8,128)(2,1)} async-done(((bf16[512,128]{1,0:T(8,128)(2,1)}), bf16[512,1024]{1,0:T(8,128)(2,1)}) %all-gather.14.cloned.1.call-update) | async-done | bytes 1048592 | tf_op jit(solution)/shard_map/all_gather | solution.py:303
  538.9 34.3 %all-reduce.54.cloned.1.call-done = f32[256,1024]{1,0:T(8,128)} async-done(((f32[256,1024]{1,0:T(8,128)}), f32[256,1024]{1,0:T(8,128)}) %all-reduce.54.cloned.1.call-update) | async-done | bytes 1048592 | tf_op jit(solution)/shard_map/psum | solution.py:379
  602.7 17.0 %while.69 = (s32[]{:T(128)}, f32[4,512,128]{2,1,0:T(8,128)}, s32[4]{0:T(128)}, s32[]{:T(128)}, bf16[2048,64]{0,1:T(8,128)(2,1)}, /*index=5*/bf16[256,2,64]{0,2,1...) while((s32[]{:T(128)}, f32[4,512,128]{2,1,0:T(8,128)}, ...), condition=%wide.region_37.39_spmd.clone, body=%wide.region_34.38_spmd.clone.sunk | while | flops 136282880 | bytes 5648669 | solution.py:420
  638.4 14.0 while.71
  679.6 40.1 %reduce-scatter.16.cloned.1.call-done = f32[256,128]{0,1:T(8,128)} async-done(((f32[2048,128]{0,1:T(8,128)}), f32[256,128]{0,1:T(8,128)}) %reduce-scatter.16.cloned.1.call-update) | async-done | bytes 131088 | tf_op jit(solution)/shard_map/reduce_scatter | solution.py:424
  730.9 18.5 %all-reduce.59 = (bf16[256,256]{1,0:T(8,128)(2,1)S(1)}, bf16[256,256]{0,1:T(8,128)(2,1)S(1)}, f32[4,256]{1,0:T(4,128)S(1)}) all-reduce(f32[256,256]{1,0:T(8,128)S(1)} %pad_maximum_fusion.2, f32[256,256]{0,1:T(8,128)} %pad_maximum_fusion.3, f32[4,256]{1,0:T(4,128)S(1)} %add_add_fusion.3), channel_id=1, replica_groups=mesh['seq'=8,'wa'=4] {'wa'}, use_global_device_ids=true, to_apply=%region_33.35 | all-reduce | flops 132096 | bytes 794624 | tf_op jit(solution)/shard_map/psum | solution.py:483
  792.5 73.4 %all-reduce.58.cloned.1.call-done = (f32[8,1024]{1,0:T(8,128)}, f32[8,4,384]{2,1,0:T(4,128)}, f32[8,4,256]{2,1,0:T(4,128)}, f32[8,6]{1,0:T(8,128)}, f32[8,6]{1,0...) async-done(((f32[8,1024]{1,0:T(8,128)}, f32[8,4,384]{2,1,0:T(4,128)}, f32[8,4,256]{2,1,0:T(4,128)}, f32[8,6]{1,0:T(8,128)}, f32[8,6]{1,0:T(8,128)}, ...) | async-done | bytes 148048
  878.8 54.3 %reduce-scatter.32.cloned.1.call-done = f32[128,128]{1,0:T(8,128)} async-done(((f32[128,1024]{1,0:T(8,128)}), f32[128,128]{1,0:T(8,128)}) %reduce-scatter.32.cloned.1.call-update) | async-done | bytes 65552 | tf_op jit(solution)/shard_map/reduce_scatter | solution.py:509
  933.1 65.6 %reduce-scatter.28.cloned.1.call-done = f32[128,128]{1,0:T(8,128)} async-done(((f32[1024,128]{1,0:T(8,128)}), f32[128,128]{1,0:T(8,128)}) %reduce-scatter.28.cloned.1.call-update) | async-done | bytes 65552 | tf_op jit(solution)/shard_map/reduce_scatter | solution.py:507
  998.7 57.4 %reduce-scatter.24.cloned.1.call-done = f32[128,6]{0,1:T(8,128)} async-done(((f32[1024,6]{0,1:T(8,128)}), f32[128,6]{0,1:T(8,128)}) %reduce-scatter.24.cloned.1.call-update) | async-done | bytes 3088 | tf_op jit(solution)/shard_map/reduce_scatter | solution.py:505
  1056.1 69.4 %reduce-scatter.26.cloned.1.call-done = f32[384,128]{1,0:T(8,128)} async-done(((f32[384,1024]{1,0:T(8,128)}), f32[384,128]{1,0:T(8,128)}) %reduce-scatter.26.cloned.1.call-update) | async-done | bytes 196624 | tf_op jit(solution)/shard_map/reduce_scatter | solution.py:506
  1125.5 68.2 %reduce-scatter.18.cloned.1.call-done = f32[128,384]{1,0:T(8,128)} async-done(((f32[1024,384]{1,0:T(8,128)}), f32[128,384]{1,0:T(8,128)}) %reduce-scatter.18.cloned.1.call-update) | async-done | bytes 196624 | tf_op jit(solution)/shard_map/reduce_scatter | solution.py:502
  1193.7 71.7 %reduce-scatter.38.cloned.1.call-done = f32[512,128]{1,0:T(8,128)} async-done(((f32[512,1024]{1,0:T(8,128)}), f32[512,128]{1,0:T(8,128)}) %reduce-scatter.38.cloned.1.call-update) | async-done | bytes 262160 | tf_op jit(solution)/shard_map/reduce_scatter | solution.py:512
  1265.4 71.3 %reduce-scatter.36.cloned.1.call-done = f32[128,512]{1,0:T(8,128)} async-done(((f32[1024,512]{1,0:T(8,128)}), f32[128,512]{1,0:T(8,128)}) %reduce-scatter.36.cloned.1.call-update) | async-done | bytes 262160 | tf_op jit(solution)/shard_map/reduce_scatter | solution.py:511
  1336.8 71.4 %reduce-scatter.34.cloned.1.call-done = f32[128,512]{1,0:T(8,128)} async-done(((f32[1024,512]{1,0:T(8,128)}), f32[128,512]{1,0:T(8,128)}) %reduce-scatter.34.cloned.1.call-update) | async-done | bytes 262160 | tf_op jit(solution)/shard_map/reduce_scatter | solution.py:510
  1408.2 67.1 %reduce-scatter.30.cloned.1.call-done = f32[128,256]{1,0:T(8,128)} async-done(((f32[1024,256]{1,0:T(8,128)}), f32[128,256]{1,0:T(8,128)}) %reduce-scatter.30.cloned.1.call-update) | async-done | bytes 131088 | tf_op jit(solution)/shard_map/reduce_scatter | solution.py:508
  1475.3 67.2 %reduce-scatter.22.cloned.1.call-done = f32[128,256]{1,0:T(8,128)} async-done(((f32[1024,256]{1,0:T(8,128)}), f32[128,256]{1,0:T(8,128)}) %reduce-scatter.22.cloned.1.call-update) | async-done | bytes 131088 | tf_op jit(solution)/shard_map/reduce_scatter | solution.py:504
  1542.5 68.5 %reduce-scatter.20.cloned.1.call-done = f32[128,384]{1,0:T(8,128)} async-done(((f32[1024,384]{1,0:T(8,128)}), f32[128,384]{1,0:T(8,128)}) %reduce-scatter.20.cloned.1.call-update) | async-done | bytes 196624 | tf_op jit(solution)/shard_map/reduce_scatter | solution.py:503
  (595 shorter events, 240.5 us)
Async XLA Ops:
  7.2 349.4 %all-gather.16.cloned.1.call-start = ((), (), s32[]{:S(2)}) async-start(), calls=%async_computation.32 | async-start | bytes 1769472 | tf_op jit(solution)/shard_map/all_gather | solution.py:26
  8.5 361.1 %copy-start.74 = (f32[256]{0:T(256)}, f32[256]{0:T(256)S(1)}, u32[]{:S(2)}) copy-start(f32[256]{0:T(256)S(1)} %add_rsqrt_fusion.1) | copy-start | bytes 3076
  43.6 194.7 %copy-start.39 = (f32[256,256]{1,0:T(8,128)}, f32[256,256]{1,0:T(8,128)S(1)}, u32[]{:S(2)}) copy-start(f32[256,256]{1,0:T(8,128)S(1)} %fusion.223) | copy-start | bytes 786436
  77.1 160.0 %copy-start.34 = (f32[256,384]{1,0:T(8,128)}, f32[256,384]{1,0:T(8,128)S(1)}, u32[]{:S(2)}) copy-start(f32[256,384]{1,0:T(8,128)S(1)} %fusion.225) | copy-start | bytes 1179652
  77.2 159.9 %collective-permute-start = (f32[3,640]{1,0:T(4,128)S(1)}, f32[3,640]{1,0:T(4,128)S(1)}, u32[]{:S(2)}, u32[]{:S(2)}) collective-permute-start(f32[3,640]{1,0:T(4,128)S(1)} %pad_maximum_fusion.10), channel_id=1, source_target_pairs={{0,4},{4,8},{8,12},{12,16},{16,20},{20,24},{24,28},{1,5},{5,9},{9,... | collective-permute-start | bytes 23048 | tf_op jit(solution)/shard_map/ppermute | solution.py:21
  81.2 157.2 %copy-start.107 = (f32[1,256]{1,0:T(1,128)}, f32[1,256]{1,0:T(1,128)S(1)}, u32[]{:S(2)}) copy-start(f32[1,256]{1,0:T(1,128)S(1)} %get-tuple-element.805) | copy-start | bytes 3076
  81.2 157.2 %copy-start.109 = (f32[1,256]{1,0:T(1,128)}, f32[1,256]{1,0:T(1,128)S(1)}, u32[]{:S(2)}) copy-start(f32[1,256]{1,0:T(1,128)S(1)} %get-tuple-element.806) | copy-start | bytes 3076
  81.2 157.2 %copy-start.111 = (f32[1,256]{1,0:T(1,128)}, f32[1,256]{1,0:T(1,128)S(1)}, u32[]{:S(2)}) copy-start(f32[1,256]{1,0:T(1,128)S(1)} %get-tuple-element.807) | copy-start | bytes 3076
  240.4 167.5 %all-reduce.52.cloned.1.call-start = ((), (), s32[]{:S(2)}) async-start(), calls=%async_computation.13 | async-start | bytes 2097152 | tf_op jit(solution)/shard_map/psum | solution.py:361
  292.7 283.1 %copy-start.43 = (bf16[2,256,64]{1,2,0:T(8,128)(2,1)}, bf16[2,256,64]{1,2,0:T(8,128)(2,1)S(1)}, u32[]{:S(2)}) copy-start(bf16[2,256,64]{1,2,0:T(8,128)(2,1)S(1)} %divide_convert_fusion) | copy-start | bytes 196612
  373.6 77.3 %all-gather.12.cloned.1.call-start = ((), (), s32[]{:S(2)}) async-start(), calls=%async_computation.15 | async-start | bytes 1179648 | tf_op jit(solution)/shard_map/all_gather | solution.py:302
  374.3 117.5 %all-gather.10.cloned.1.call-start = ((), (), s32[]{:S(2)}) async-start(), calls=%async_computation.14 | async-start | bytes 1179648 | tf_op jit(solution)/shard_map/all_gather | solution.py:301
  374.9 157.0 %all-gather.14.cloned.1.call-start = ((), (), s32[]{:S(2)}) async-start(), calls=%async_computation.16 | async-start | bytes 1179648 | tf_op jit(solution)/shard_map/all_gather | solution.py:303
  375.5 197.7 %all-reduce.54.cloned.1.call-start = ((), (), s32[]{:S(2)}) async-start(), calls=%async_computation.18 | async-start | bytes 2097152 | tf_op jit(solution)/shard_map/psum | solution.py:379
  409.4 166.1 %copy-start.90 = (f32[256]{0:T(256)}, f32[256]{0:T(256)S(1)}, u32[]{:S(2)}) copy-start(f32[256]{0:T(256)S(1)} %add_rsqrt_fusion) | copy-start | bytes 3076
  537.8 100.6 %all-gather.18.cloned.1.call-start = ((), (), s32[]{:S(2)}) async-start(), calls=%async_computation.33 | async-start | bytes 1769472 | tf_op jit(solution)/shard_map/all_gather | solution.py:26
  584.9 134.8 %reduce-scatter.16.cloned.1.call-start = ((), (), s32[]{:S(2)}) async-start(), calls=%async_computation.20 | async-start | bytes 1179648 | tf_op jit(solution)/shard_map/reduce_scatter | solution.py:424
  628.3 131.5 %all-reduce.56.cloned.1.call-start = ((), (), s32[]{:S(2)}) async-start(), calls=%async_computation.19 | async-start | bytes 2097152 | tf_op jit(solution)/shard_map/psum | solution.py:483
  667.8 5.6 collective-permute-start.1
  675.3 112.9 %reduce-scatter.14.cloned.1.call-start = ((), (), s32[]{:S(2)}) async-start(), calls=%async_computation.17 | async-start | bytes 1310720 | tf_op jit(solution)/shard_map/reduce_scatter | solution.py:368
  678.8 187.2 %all-reduce.58.cloned.1.call-start = ((), (), s32[]{:S(2)}) async-start(), calls=%async_computation.34 | async-start | bytes 319488
  767.5 165.6 %reduce-scatter.32.cloned.1.call-start = ((), (), s32[]{:S(2)}) async-start(), calls=%async_computation.28 | async-start | bytes 589824 | tf_op jit(solution)/shard_map/reduce_scatter | solution.py:509
  768.6 230.1 %reduce-scatter.28.cloned.1.call-start = ((), (), s32[]{:S(2)}) async-start(), calls=%async_computation.26 | async-start | bytes 589824 | tf_op jit(solution)/shard_map/reduce_scatter | solution.py:507
  769.9 286.2 %reduce-scatter.24.cloned.1.call-start = ((), (), s32[]{:S(2)}) async-start(), calls=%async_computation.24 | async-start | bytes 36864 | tf_op jit(solution)/shard_map/reduce_scatter | solution.py:505
  770.9 354.5 %reduce-scatter.26.cloned.1.call-start = ((), (), s32[]{:S(2)}) async-start(), calls=%async_computation.25 | async-start | bytes 1769472 | tf_op jit(solution)/shard_map/reduce_scatter | solution.py:506
  772.7 421.0 %reduce-scatter.18.cloned.1.call-start = ((), (), s32[]{:S(2)}) async-start(), calls=%async_computation.21 | async-start | bytes 1769472 | tf_op jit(solution)/shard_map/reduce_scatter | solution.py:502
  774.5 491.0 %reduce-scatter.38.cloned.1.call-start = ((), (), s32[]{:S(2)}) async-start(), calls=%async_computation.31 | async-start | bytes 2359296 | tf_op jit(solution)/shard_map/reduce_scatter | solution.py:512
  776.4 560.4 %reduce-scatter.36.cloned.1.call-start = ((), (), s32[]{:S(2)}) async-start(), calls=%async_computation.30 | async-start | bytes 2359296 | tf_op jit(solution)/shard_map/reduce_scatter | solution.py:511
  779.3 628.9 %reduce-scatter.34.cloned.1.call-start = ((), (), s32[]{:S(2)}) async-start(), calls=%async_computation.29 | async-start | bytes 2359296 | tf_op jit(solution)/shard_map/reduce_scatter | solution.py:510
  782.1 693.3 %reduce-scatter.30.cloned.1.call-start = ((), (), s32[]{:S(2)}) async-start(), calls=%async_computation.27 | async-start | bytes 1179648 | tf_op jit(solution)/shard_map/reduce_scatter | solution.py:508
  783.6 758.9 %reduce-scatter.22.cloned.1.call-start = ((), (), s32[]{:S(2)}) async-start(), calls=%async_computation.23 | async-start | bytes 1179648 | tf_op jit(solution)/shard_map/reduce_scatter | solution.py:504
  785.1 825.9 %reduce-scatter.20.cloned.1.call-start = ((), (), s32[]{:S(2)}) async-start(), calls=%async_computation.22 | async-start | bytes 1769472 | tf_op jit(solution)/shard_map/reduce_scatter | solution.py:503
  (129 other events, 2811.0 us)
Sparse Core Ops, SparseCore 0:
  240.6 44.2 all-gather.15
  373.7 34.2 all-reduce.51
  410.1 40.7 all-gather.11
  452.9 38.9 all-gather.9
  493.8 38.0 all-gather.13
  537.9 35.2 all-reduce.53
  585.0 53.2 all-gather.17
  641.7 77.9 reduce-scatter.15
  722.0 37.7 all-reduce.55
  762.8 25.3 reduce-scatter.13
  794.1 71.8 all-reduce.57
  869.8 63.2 reduce-scatter.31
  937.0 61.6 reduce-scatter.27
  1002.2 53.8 reduce-scatter.23
  1060.0 65.4 reduce-scatter.25
  1129.3 64.3 reduce-scatter.17
  1197.7 67.7 reduce-scatter.37
  1269.4 67.3 reduce-scatter.35
  1340.9 67.2 reduce-scatter.33
  1412.0 63.2 reduce-scatter.29
  1479.3 63.1 reduce-scatter.21
  1546.5 64.4 reduce-scatter.19
where the time goes:
time: 1630 us; the launch traced here: 1620 us
  waiting for transfers between devices  1050 us (64%)
  blocking collectives  344 us (21%)
  matrix products  73.6 us (5%)
  other arithmetic  61.7 us (4%)
  local copies, waits for them, and re-layouts  54.4 us (3%)
  between operations  16.6 us (1%)
  starting transfers between devices  16.3 us (1%)
    unnamed x23, waiting for transfers between devices  75.5 us
    reduce_scatter x1, waiting for transfers between devices, per_device(): lax.psum_scatter(part_w_down, 'seq', scatter_dimension=1, tiled=True)  71.7 us
    reduce_scatter x1, waiting for transfers between devices, per_device(): lax.psum_scatter(part_w_gate, 'seq', scatter_dimension=0, tiled=True)  71.4 us
    reduce_scatter x1, waiting for transfers between devices, per_device(): lax.psum_scatter(part_w_up, 'seq', scatter_dimension=0, tiled=True)  71.3 us
    reduce_scatter x1, waiting for transfers between devices, per_device(): lax.psum_scatter(part_w_out, 'seq', scatter_dimension=1, tiled=True)  69.4 us
    reduce_scatter x1, waiting for transfers between devices, per_device(): lax.psum_scatter(part_w_x, 'seq', scatter_dimension=0, tiled=True)  68.5 us
    reduce_scatter x1, waiting for transfers between devices, per_device(): lax.psum_scatter(part_w_z, 'seq', scatter_dimension=0, tiled=True)  68.2 us
    reduce_scatter x1, waiting for transfers between devices, per_device(): lax.psum_scatter(part_w_bc, 'seq', scatter_dimension=0, tiled=True)  67.2 us
  transfers between devices with their start and end apart: 24, of which 21 were waited for; matrix products, arithmetic and copies ran while one was open for 9% of the time, Pallas kernels for 0%

commit v1 on v0

v1 whole, which is shorter than its diff:
```python
import jax
import jax.numpy as jnp
from jax import lax
from jax.sharding import PartitionSpec as P

NS = 128
CONVK = 4
QH = 8
KVH = 2
HD = 64


EPS = 1e-05
ROPE_BASE = 100000000000.0
highest = lax.Precision.HIGHEST


def passed_along(value, axis, steps):
    count = lax.axis_size(axis)
    leading, last = (max(0, -steps), min(count, count - steps))
    return lax.ppermute(value, axis, [(source, source + steps) for source in range(leading, last)])


def project(left_side, right_side):
    return jnp.dot(left_side, right_side, preferred_element_type=jnp.float32)


def rms_scale(row_values):
    return lax.rsqrt(jnp.mean(row_values * row_values, axis=-1, keepdims=True) + EPS)


def rope_tables(positions):
    frequency = ROPE_BASE ** (-(jnp.arange(HD // 2, dtype=jnp.float32) * 2.0 / HD))
    angles = positions.astype(jnp.float32)[:, None] * frequency[None, :]
    return (jnp.cos(angles), jnp.sin(angles))


def rotate(values, cosine, sine):
    half_width = values.shape[-1] // 2
    first_half = values[..., :half_width]
    second_half = values[..., half_width:]
    cos_part = cosine[:, None, :]
    sin_part = sine[:, None, :]
    return jnp.concatenate(
        [
            first_half * cos_part - second_half * sin_part,
            second_half * cos_part + first_half * sin_part,
        ],
        axis=-1,
    )


def unrotate(gradients, cosine, sine):
    half_width = gradients.shape[-1] // 2
    first_half = gradients[..., :half_width]
    second_half = gradients[..., half_width:]
    cos_part = cosine[:, None, :]
    sin_part = sine[:, None, :]
    return jnp.concatenate(
        [
            first_half * cos_part + second_half * sin_part,
            second_half * cos_part - first_half * sin_part,
        ],
        axis=-1,
    )


HALO = 16
SUM_TYPE = jnp.bfloat16
LANES = 128


def rounded_up(width):
    return -(-width // LANES) * LANES


def prepare(x_rows, bc_rows, dt_input, conv_x, conv_bc, dt_bias, a_log):
    length, head_count = dt_input.shape

    def conv_silu(padded, kernel):
        first = padded.shape[0] - length - CONVK + 1
        running = kernel[0] * padded[first : first + length]
        for offset in range(1, CONVK):
            running = running + kernel[offset] * padded[first + offset : first + offset + length]
        return jax.nn.silu(running)

    x_heads = conv_silu(x_rows, conv_x).reshape(length, head_count, -1).transpose(1, 0, 2)
    bc_conv = conv_silu(bc_rows, conv_bc)
    step_size = jax.nn.softplus(dt_input + dt_bias[None, :]).T
    log_decay = -jnp.exp(a_log)[:, None] * step_size
    ticks = jnp.arange(length, dtype=jnp.int32)
    upto = (ticks[:, None] <= ticks[None, :]).astype(jnp.float32)
    cumulative = jnp.dot(log_decay, upto, precision=highest)
    return (x_heads, bc_conv[:, :NS], bc_conv[:, NS:], step_size, cumulative)


def ssd_state(x_heads, b_mat, step_size, cumulative):
    tail_weight = jnp.exp(cumulative[:, -1:] - cumulative) * step_size
    local_state = jnp.einsum(
        "hsp,sn->hpn", x_heads * tail_weight[:, :, None], b_mat, precision=highest
    )
    return (cumulative[:, -1], local_state)


def ssd_gated(z_input, x_heads, b_mat, c_mat, step_size, cumulative, d_skip, start_state):
    head_count, length, _ = x_heads.shape
    ticks = jnp.arange(length, dtype=jnp.int32)
    causal = ticks[:, None] >= ticks[None, :]
    gap_sums = cumulative[:, :, None] - cumulative[:, None, :]
    decays = jnp.exp(jnp.where(causal[None], gap_sums, -1e30))
    intersections = lax.dot_general(c_mat, b_mat, (((1,), (1,)), ((), ())), precision=highest)
    mixing = decays * intersections[None] * step_size[:, None, :]
    inner_part = jnp.einsum("hts,hsp->htp", mixing, x_heads, precision=highest)
    carried = (
        jnp.einsum("tn,hpn->htp", c_mat, start_state, precision=highest)
        * jnp.exp(cumulative)[:, :, None]
    )
    ssm_out = inner_part + carried + d_skip[:, None, None] * x_heads
    return ssm_out.transpose(1, 0, 2).reshape(length, -1) * jax.nn.silu(z_input)


def times(left_side, right_side, left_dim, right_dim):
    return lax.dot_general(
        left_side,
        right_side,
        (((left_dim,), (right_dim,)), ((), ())),
        preferred_element_type=jnp.float32,
    )


def split_columns(packed, widths):
    pieces, at = ([], 0)
    for width in widths:
        pieces.append(packed[:, at : at + width])
        at += rounded_up(width)
    return pieces


def padded_columns(values):
    return jnp.pad(values, ((0, 0), (0, rounded_up(values.shape[1]) - values.shape[1])))


def pack_columns(pieces):
    return jnp.concatenate([padded_columns(piece) for piece in pieces], axis=1)


def seq_gather(values):
    return lax.all_gather(values, "seq", axis=0, tiled=False)


def seq_reduce(values):
    return lax.psum_scatter(values, "seq", scatter_dimension=0, tiled=False)


def grads_reduce(values):
    return lax.psum_scatter(values, "seq", scatter_dimension=0, tiled=True)


def wa_sum(values):
    return lax.psum(values, "wa")


def split_three(values):
    high = values.astype(jnp.bfloat16)
    left = values - lax.reduce_precision(values, 8, 7)
    middle = left.astype(jnp.bfloat16)
    low = (left - lax.reduce_precision(left, 8, 7)).astype(jnp.bfloat16)
    return (high, middle, low)


def per_device(
    tokens,
    gain_mix,
    w_z,
    w_x,
    w_bc,
    w_dt,
    conv_x,
    conv_bc,
    dt_bias,
    a_log,
    d_skip,
    w_out,
    w_q,
    w_kv,
    w_o,
    gain_ffn,
    w_gate,
    w_up,
    w_down,
    cotangent,
):
    rows, width = tokens.shape
    seq_count = lax.axis_size("seq")
    seq_index = lax.axis_index("seq")
    wa_index = lax.axis_index("wa")
    head_count = a_log.shape[0]
    state_rows = head_count * (w_x.shape[1] // head_count)
    before = passed_along(tokens[rows - HALO :], "seq", 1)
    weights = (w_z, w_x, w_bc, w_q, w_kv, w_dt, w_gate, w_up, w_out.T, w_o.T, w_down.T)
    widths = [w.shape[1] for w in weights]
    first_width = sum(rounded_up(w) for w in widths[:6])
    gate_width = first_width + widths[6] + widths[7]
    mixed_width = gate_width + widths[8] + widths[9]
    full = lax.all_gather(pack_columns(weights), "seq", axis=0, tiled=True)
    full_first = full[:, :first_width]
    full_ffn = full[:, first_width:gate_width]
    full_mixed = full[:, gate_width:mixed_width]
    full_down = full[:, mixed_width:]

    def normalised(values):
        wide = values.astype(jnp.float32)
        return (wide * rms_scale(wide) * gain_mix).astype(jnp.bfloat16)

    tokens_wide = tokens.astype(jnp.float32)
    scale_mix = rms_scale(tokens_wide)
    normed = (tokens_wide * scale_mix * gain_mix).astype(jnp.bfloat16)
    extended = jnp.concatenate([normalised(before), normed], axis=0)
    projected = project(extended, full_first)
    z_rows, x_rows, bc_rows, q_rows, kv_rows, dt_rows = split_columns(projected, widths[:6])
    z_proj = z_rows[HALO:]
    mixer_inputs = (x_rows, bc_rows, dt_rows[HALO:], conv_x, conv_bc, dt_bias, a_log)
    prepared, pull_prepare = jax.vjp(prepare, *mixer_inputs)
    x_heads, b_mat, c_mat, step_size, cumulative = prepared
    (log_total, local_state), pull_state = jax.vjp(
        ssd_state, x_heads, b_mat, step_size, cumulative
    )

    local_query = w_q.shape[1] // HD
    kv_head = wa_index * local_query // (QH // KVH)
    positions = seq_index * rows + jnp.arange(rows, dtype=jnp.int32)
    cosine, sine = rope_tables(positions)
    q_proj = q_rows[HALO:].reshape(rows, local_query, HD)
    kv_proj = kv_rows[HALO:]
    k_proj = lax.dynamic_slice_in_dim(kv_proj, kv_head * HD, HD, 1)
    v_proj = lax.dynamic_slice_in_dim(kv_proj, KVH * HD + kv_head * HD, HD, 1)
    q_rot = rotate(q_proj, cosine, sine).astype(jnp.bfloat16).transpose(1, 0, 2)
    k_rot = rotate(k_proj[:, None, :], cosine, sine)[:, 0, :]
    total_rows = jnp.pad(
        jnp.stack(split_three(log_total)), ((0, HALO - 3), (0, LANES - head_count))
    )
    sent = jnp.concatenate(
        [
            jnp.concatenate([k_rot, v_proj], axis=1).astype(jnp.bfloat16),
            local_state.reshape(state_rows, NS).astype(jnp.bfloat16),
            total_rows,
        ],
        axis=0,
    )
    arrived = seq_gather(sent)
    key_all = arrived[:, :rows, :HD].reshape(seq_count * rows, HD)
    value_all = arrived[:, :rows, HD:].reshape(seq_count * rows, HD)
    states = arrived[:, rows : rows + state_rows].astype(jnp.float32)
    totals = jnp.sum(
        arrived[:, rows + state_rows : rows + state_rows + 3, :head_count].astype(jnp.float32),
        axis=1,
    )
    blocks = jnp.arange(seq_count, dtype=jnp.int32)
    low_end = jnp.minimum(blocks, seq_index)
    high_end = jnp.maximum(blocks, seq_index)
    between = (blocks[None, :] > low_end[:, None]) & (blocks[None, :] < high_end[:, None])
    path_decay = jnp.exp(jnp.sum(jnp.where(between[:, :, None], totals[None], 0.0), axis=1))
    earlier = jnp.where((blocks < seq_index)[:, None], path_decay, 0.0)
    later = jnp.where((blocks < seq_index)[:, None], path_decay, 0.0)
    shape_all = (seq_count, head_count, state_rows // head_count, NS)
    start_state = jnp.sum(earlier[:, :, None, None] * states.reshape(shape_all), axis=0)
    ssm_gated, pull_output = jax.vjp(
        ssd_gated, z_proj, x_heads, b_mat, c_mat, step_size, cumulative, d_skip, start_state
    )
    gated = ssm_gated.astype(jnp.bfloat16)

    key_pos = jnp.arange(seq_count * rows, dtype=jnp.int32)
    allowed = (key_pos[None, :] <= positions[:, None])[None]

    def per_head(left_side, right_side, left_dim, right_dim):
        return jnp.stack(
            [times(left_side[g], right_side, left_dim, right_dim) for g in range(local_query)]
        )

    scores = jnp.where(allowed, per_head(q_rot, key_all, 1, 1) * HD ** (-0.5), -1e30)
    row_max = jnp.max(scores, axis=-1, keepdims=True)
    attn_weights = jnp.exp(scores - row_max)
    row_sum = jnp.sum(attn_weights, axis=-1, keepdims=True)
    weighted_sum = per_head(attn_weights.astype(jnp.bfloat16), value_all, 1, 0)
    attn_heads = (weighted_sum / row_sum).astype(jnp.bfloat16)
    log_sums = row_max + jnp.log(row_sum)
    attn_out = attn_heads.transpose(1, 0, 2).reshape(rows, local_query * HD)
    mixed = jnp.concatenate([gated, attn_out], axis=1)
    hidden = tokens_wide + wa_sum(times(mixed, full_mixed, 1, 1))
    scale_ffn = rms_scale(hidden)
    hnormed = (hidden * scale_ffn * gain_ffn).astype(jnp.bfloat16)
    ffn_width = widths[6]
    ffn_proj = project(hnormed, full_ffn)
    gate_proj = ffn_proj[:, :ffn_width]
    up_proj = ffn_proj[:, ffn_width:]
    activated = (jax.nn.silu(gate_proj) * up_proj).astype(jnp.bfloat16)
    ffn_part = times(activated, full_down, 1, 1)
    cot_wide = cotangent.astype(jnp.float32)
    d_act = project(cotangent, full_down)
    sigmoid_gate = jax.nn.sigmoid(gate_proj)
    d_gate = d_act * up_proj * sigmoid_gate * (1.0 + gate_proj * (1.0 - sigmoid_gate))
    d_up = d_act * gate_proj * sigmoid_gate
    d_ffn = jnp.concatenate([d_gate.astype(jnp.bfloat16), d_up.astype(jnp.bfloat16)], axis=1)
    d_hnormed = wa_sum(times(d_ffn, full_ffn, 1, 1))
    hidden_hat = hidden * scale_ffn
    weighted_ffn = d_hnormed * gain_ffn
    d_hidden = cot_wide + scale_ffn * (
        weighted_ffn - hidden_hat * jnp.mean(weighted_ffn * hidden_hat, axis=-1, keepdims=True)
    )
    grad_gain_ffn = jnp.sum(d_hnormed * hidden_hat, axis=0)
    d_hidden_b = d_hidden.astype(jnp.bfloat16)
    d_mixed = project(d_hidden_b, full_mixed)
    inner_width = widths[8]
    d_gated = d_mixed[:, :inner_width]
    d_attn_heads = (
        d_mixed[:, inner_width:]
        .astype(jnp.bfloat16)
        .reshape(rows, local_query, HD)
        .transpose(1, 0, 2)
    )
    out_grads = pull_output(d_gated)
    direct = out_grads[7]
    out_delta = jnp.sum(
        d_attn_heads.astype(jnp.float32) * attn_heads.astype(jnp.float32), axis=-1, keepdims=True
    )
    probability = jnp.exp(scores - log_sums)
    d_probs = per_head(d_attn_heads, value_all, 1, 1)
    d_scores = (probability * (d_probs - out_delta)).astype(jnp.bfloat16)
    flat_rows = (local_query * rows, -1)
    d_key = times(d_scores.reshape(flat_rows), q_rot.reshape(flat_rows), 0, 0) * HD ** (-0.5)
    d_value = times(
        probability.astype(jnp.bfloat16).reshape(flat_rows), d_attn_heads.reshape(flat_rows), 0, 0
    )
    key_parts = jnp.concatenate([d_key, d_value], axis=1).reshape(seq_count, rows, 2 * HD)
    state_parts = (later[:, :, None, None] * direct[None]).reshape(seq_count, state_rows, NS)
    own_parts = seq_reduce(
        jnp.concatenate([key_parts, state_parts], axis=1).astype(SUM_TYPE)
    ).astype(jnp.float32)
    d_q_rot = per_head(d_scores, key_all, 1, 0) * HD ** (-0.5)
    d_q = unrotate(d_q_rot.transpose(1, 0, 2), cosine, sine).reshape(rows, -1).astype(jnp.bfloat16)
    d_key_own = unrotate(own_parts[:rows, None, :HD], cosine, sine)[:, 0, :]
    d_value_own = own_parts[:rows, HD:]
    d_end = own_parts[rows:].reshape(direct.shape)
    d_total = jnp.exp(log_total) * jnp.sum(d_end * start_state, axis=(1, 2))
    state_grads = pull_state((d_total, d_end))
    merged = (
        out_grads[1] + state_grads[0],
        out_grads[2] + state_grads[1],
        out_grads[3],
        out_grads[4] + state_grads[2],
        out_grads[5] + state_grads[3],
    )
    (
        d_x_rows,
        d_bc_rows,
        d_dt_in,
        grad_conv_x,
        grad_conv_bc,
        grad_dt_bias,
        grad_a_log,
    ) = pull_prepare(merged)
    x_width = widths[1]
    edge_back = passed_along(
        jnp.concatenate([d_x_rows[:HALO], d_bc_rows[:HALO]], axis=1), "seq", -1
    )
    d_x_in = d_x_rows[HALO:].at[rows - HALO :].add(edge_back[:, :x_width])
    d_bc_in = d_bc_rows[HALO:].at[rows - HALO :].add(edge_back[:, x_width:])
    d_z_b = out_grads[0].astype(jnp.bfloat16)
    d_x_b = d_x_in.astype(jnp.bfloat16)
    d_dt_b = d_dt_in.astype(jnp.bfloat16)
    head_pick = (jnp.arange(KVH, dtype=jnp.int32) == kv_head).astype(jnp.float32)
    d_kv_part = jnp.concatenate(
        [head_pick[k] * part for part in (d_key_own, d_value_own) for k in range(KVH)], axis=1
    )
    full_z, full_x, full_bc, full_q, full_kv, full_dt = split_columns(full_first, widths[:6])
    d_normed_part = (
        times(jnp.concatenate([d_z_b, d_x_b], axis=1), full[:, : widths[0] + x_width], 1, 1)
        + times(d_dt_b, full_dt, 1, 1)
        + times(d_q, full_q, 1, 1)
    )
    shared = jnp.concatenate([d_normed_part, d_bc_in, d_kv_part], axis=1)
    conv_rows = jnp.pad(
        grad_conv_bc, ((0, 8 - CONVK), (0, shared.shape[1] - grad_conv_bc.shape[1]))
    )
    shared = wa_sum(jnp.concatenate([shared, conv_rows], axis=0))
    d_normed_sum = shared[:rows, :width]
    d_bckv_b = shared[:rows, width:].astype(jnp.bfloat16)
    grad_conv_bc = shared[rows : rows + CONVK, : grad_conv_bc.shape[1]]
    d_bc_b = d_bckv_b[:, : widths[2]]
    d_kv_b = d_bckv_b[:, widths[2] :]
    d_normed = d_normed_sum + times(d_bc_b, full_bc, 1, 1) + times(d_kv_b, full_kv, 1, 1)
    tokens_hat = tokens_wide * scale_mix
    weighted_mix = d_normed * gain_mix
    grad_tokens = d_hidden + scale_mix * (
        weighted_mix - tokens_hat * jnp.mean(weighted_mix * tokens_hat, axis=-1, keepdims=True)
    )
    grad_gain_mix = jnp.sum(d_normed * tokens_hat, axis=0)
    ffn_own = lax.psum_scatter(ffn_part, "wa", scatter_dimension=1, tiled=True)
    own_width = ffn_own.shape[1]
    hidden_own = lax.dynamic_slice_in_dim(hidden, wa_index * own_width, own_width, 1)
    output = (hidden_own + ffn_own).astype(jnp.bfloat16)
    d_first = pack_columns([d_z_b, d_x_b, d_bc_b, d_q, d_kv_b, d_dt_b])
    parts = jnp.concatenate(
        [
            times(normed, d_first, 0, 0).astype(SUM_TYPE),
            times(hnormed, d_ffn, 0, 0).astype(SUM_TYPE),
            times(d_hidden_b, mixed, 0, 0).astype(SUM_TYPE),
            times(cotangent, activated, 0, 0).astype(SUM_TYPE),
        ],
        axis=1,
    )
    own = grads_reduce(parts).astype(jnp.float32)
    grads = split_columns(own, widths)
    small = (
        grad_gain_mix,
        grad_gain_ffn,
        grad_conv_x.reshape(-1),
        grad_conv_bc.reshape(-1),
        grad_dt_bias,
        grad_a_log,
        out_grads[6],
    )
    small_sum = lax.psum(jnp.concatenate(small), "seq")
    sums, at = ([], 0)
    for piece in small:
        sums.append(small_sum[at : at + piece.shape[0]])
        at += piece.shape[0]
    return (
        output,
        grad_tokens,
        sums[0],
        grads[0],
        grads[1],
        grads[2],
        grads[5],
        sums[2].reshape(conv_x.shape),
        sums[3].reshape(conv_bc.shape),
        sums[4],
        sums[5],
        sums[6],
        grads[8].T,
        grads[3],
        grads[4],
        grads[9].T,
        sums[1],
        grads[6],
        grads[7],
        grads[10].T,
    )


def solution(mesh):
    placed = (
        P("seq", None),
        P(),
        P("seq", "wa"),
        P("seq", "wa"),
        P("seq", None),
        P("seq", "wa"),
        P(None, "wa"),
        P(),
        P("wa"),
        P("wa"),
        P("wa"),
        P("wa", "seq"),
        P("seq", "wa"),
        P("seq", None),
        P("wa", "seq"),
        P(),
        P("seq", "wa"),
        P("seq", "wa"),
        P("wa", "seq"),
        P("seq", None),
    )
    return jax.shard_map(
        per_device,
        mesh=mesh,
        in_specs=placed,
        out_specs=(
            P("seq", "wa"),
            P("seq", None),
            P(),
            P("seq", "wa"),
            P("seq", "wa"),
            P("seq", None),
            P("seq", "wa"),
            P(None, "wa"),
            P(),
            P("wa"),
            P("wa"),
            P("wa"),
            P("wa", "seq"),
            P("seq", "wa"),
            P("seq", None),
            P("wa", "seq"),
            P(),
            P("seq", "wa"),
            P("seq", "wa"),
            P("wa", "seq"),
        ),
        check_vma=False,
    )
```

time: 1630 us -> 658 us (0.40)
  waiting for transfers between devices: 1050 us -> 409 us
  blocking collectives: 344 us -> 39.3 us
    reduce_scatter x13 -> x3, waiting for transfers between devices: 773 us -> 160 us  [the longest x1 87.8 us: grads_reduce(): return lax.psum_scatter(values, 'seq', scatter_dimension=0, tiled=True)]
    all_gather x11 -> x0, blocking collectives: 326 us -> none  [the longest x1 33.7 us: per_device(): lax.all_gather(w_z, 'seq', axis=0, tiled=True)]
    unnamed x23 -> x8, waiting for transfers between devices: 75.5 us -> 0.13 us
    dot_general x33 -> x4, matrix products: 48.2 us -> 9.67 us  [project(): return jnp.dot(left_side, right_side, preferred_element_type=jnp.float32)]
    dot_general x19 -> x36, matrix products: 25.4 us -> 57.7 us  [the longest x22 36.5 us: times(): lax.dot_general(left_side, right_side, (((left_dim,), (right_dim,)), ((),...]
    all_gather x5 -> x2, waiting for transfers between devices: 117 us -> 144 us  [the longest x1 108 us: per_device(): full = lax.all_gather(pack_columns(weights), 'seq', axis=0, tiled=True)]
    psum x3, waiting for transfers between devices: 76.9 us -> 103 us  [wa_sum(): return lax.psum(values, 'wa')]
    psum x1, blocking collectives: 18.5 us -> 39.3 us  [per_device(): small_sum = lax.psum(jnp.concatenate(small), 'seq')]
  transfers between devices with their start and end apart: 24 -> 10, of which waited for: 21 -> 9; matrix products, arithmetic and copies ran while one was open for 9% -> 9% of each run, Pallas kernels for 0% -> 0%
where the time goes in v1:
time: 658 us; the launch traced here: 647 us
  waiting for transfers between devices  409 us (62%)
  matrix products  67.4 us (10%)
  local copies, waits for them, and re-layouts  56 us (9%)
  other arithmetic  51.6 us (8%)
  blocking collectives  39.3 us (6%)
  between operations  16.9 us (3%)
  starting transfers between devices  7.12 us (1%)
    all_gather x1, waiting for transfers between devices, per_device(): full = lax.all_gather(pack_columns(weights), 'seq', axis=0, tiled=True)  108 us
    psum x3, waiting for transfers between devices, wa_sum(): return lax.psum(values, 'wa')  103 us
    reduce_scatter x1, waiting for transfers between devices, grads_reduce(): return lax.psum_scatter(values, 'seq', scatter_dimension=0, tiled=True)  87.8 us
    reduce_scatter x1, waiting for transfers between devices, seq_reduce(): return lax.psum_scatter(values, 'seq', scatter_dimension=0, tiled=False)  52.6 us
    psum x1, blocking collectives, per_device(): small_sum = lax.psum(jnp.concatenate(small), 'seq')  39.3 us
    dot_general x22, matrix products, times(): lax.dot_general(left_side, right_side, (((left_dim,), (right_dim,)), ((),...  36.5 us
    all_gather x1, waiting for transfers between devices, seq_gather(): return lax.all_gather(values, 'seq', axis=0, tiled=False)  35.9 us
    unnamed x336, local copies, waits for them, and re-layouts  25.9 us
  transfers between devices with their start and end apart: 10, of which 9 were waited for; matrix products, arithmetic and copies ran while one was open for 9% of the time, Pallas kernels for 0%

profile of v1, /device:TPU:0, one launch (start us, length us, event | category | flops | bytes accessed | tf_op | source)
XLA Modules:
  0.0 647.2 jit_solution(6879466185800236030)
XLA Ops:
  16.3 4.9 collective-permute-start
  23.0 108.3 %all-gather.4.cloned.1.call-done = bf16[1024,3584]{0,1:T(8,128)(2,1)} async-done(((bf16[128,3584]{0,1:T(8,128)(2,1)}), bf16[1024,3584]{0,1:T(8,128)(2,1)}) %all-gather.4.cloned.1.call-update) | async-done | bytes 7340048 | tf_op jit(solution)/shard_map/all_gather | solution.py:205
  131.2 3.0 fusion.6
  144.0 35.9 %all-gather.6.cloned.1.call-done = bf16[5248,128]{1,0:T(8,128)(2,1)} async-done(((bf16[656,128]{1,0:T(8,128)(2,1)}), bf16[5248,128]{1,0:T(8,128)(2,1)}) %all-gather.6.cloned.1.call-update) | async-done | bytes 1343504 | tf_op jit(solution)/shard_map/all_gather | solution.py:148
  179.9 2.2 slice.457
  188.7 2.4 copy.344
  194.0 3.8 fusion.48
  201.1 2.7 fusion.66
  204.0 35.0 %all-reduce.28.cloned.1.call-done = f32[256,1024]{1,0:T(8,128)} async-done(((f32[256,1024]{1,0:T(8,128)}), f32[256,1024]{1,0:T(8,128)}) %all-reduce.28.cloned.1.call-update) | async-done | bytes 1048592 | tf_op jit(solution)/shard_map/psum | solution.py:160
  240.7 2.4 fusion.15
  243.1 2.6 multiply_convert_fusion.3
  246.5 3.3 fusion.13
  251.2 35.5 %all-reduce.30.cloned.1.call-done = f32[256,1024]{1,0:T(8,128)} async-done(((f32[256,1024]{1,0:T(8,128)}), f32[256,1024]{1,0:T(8,128)}) %all-reduce.30.cloned.1.call-update) | async-done | bytes 1048592 | tf_op jit(solution)/shard_map/psum | solution.py:160
  286.7 2.3 multiply_reduce_fusion.3
  298.2 2.1 slice_multiply_fusion
  307.5 2.5 pad_maximum_fusion.1
  315.1 3.2 fusion.69
  320.0 2.2 fusion.106
  323.2 52.6 %reduce-scatter.6.cloned.1.call-done = bf16[1,640,128]{1,2,0:T(8,128)(2,1)} async-done(((bf16[8,640,128]{1,2,0:T(8,128)(2,1)}), bf16[1,640,128]{1,2,0:T(8,128)(2,1)}) %reduce-scatter.6.cloned.1.call-update) | async-done | bytes 163856 | tf_op jit(solution)/shard_map/reduce_scatter | solution.py:152
  378.4 2.8 multiply_reduce_fusion.6
  383.9 2.2 fusion.204
  386.1 3.7 fusion.51
  399.0 2.9 slice_multiply_fusion.1
  416.1 3.2 fusion.33
  423.9 2.6 fusion.62
  426.5 3.3 convolution_convert_fusion.1
  431.5 2.3 convolution_convert_fusion.3
  434.7 32.6 %all-reduce.32.cloned.1.call-done = f32[264,1536]{1,0:T(8,128)} async-done(((f32[264,1536]{1,0:T(8,128)}), f32[264,1536]{1,0:T(8,128)}) %all-reduce.32.cloned.1.call-update) | async-done | bytes 1622032 | tf_op jit(solution)/shard_map/psum | solution.py:160
  471.8 3.3 pad_maximum_fusion
  475.2 20.1 %reduce-scatter.4.cloned.1.call-done = f32[256,256]{1,0:T(8,128)} async-done(((f32[256,1024]{1,0:T(8,128)}), f32[256,256]{1,0:T(8,128)}) %reduce-scatter.4.cloned.1.call-update) | async-done | bytes 262160 | tf_op jit(solution)/shard_map/reduce_scatter | solution.py:398
  501.5 39.3 %psum.31 = f32[4626]{0:T(1024)S(1)} all-reduce(f32[4626]{0:T(1024)S(1)} %concatenate.83), channel_id=1, replica_groups=mesh['seq'=8,'wa'=4] {'seq'}, use_global_device_ids=true, to_apply=%region_38.39 | all-reduce | flops 4626 | bytes 37008 | tf_op jit(solution)/shard_map/psum | solution.py:423
  544.5 87.8 %reduce-scatter.8.cloned.1.call-done = bf16[128,3584]{1,0:T(8,128)(2,1)} async-done(((bf16[1024,3584]{1,0:T(8,128)(2,1)}), bf16[128,3584]{1,0:T(8,128)(2,1)}) %reduce-scatter.8.cloned.1.call-update) | async-done | bytes 917520 | tf_op jit(solution)/shard_map/reduce_scatter | solution.py:156
  (518 shorter events, 117.4 us)
Async XLA Ops:
  7.2 124.0 %all-gather.4.cloned.1.call-start = ((), (), s32[]{:S(2)}) async-start(), calls=%async_computation.3 | async-start | bytes 8257536 | tf_op jit(solution)/shard_map/all_gather | solution.py:205
  16.2 163.7 %all-gather.6.cloned.1.call-start = ((), (), s32[]{:S(2)}) async-start(), calls=%async_computation.10 | async-start | bytes 1511424 | tf_op jit(solution)/shard_map/all_gather | solution.py:148
  16.3 6.5 collective-permute-start
  21.2 120.2 %copy-start.112 = (f32[256]{0:T(256)}, f32[256]{0:T(256)S(1)}, u32[]{:S(2)}) copy-start(f32[256]{0:T(256)S(1)} %get-tuple-element.288) | copy-start | bytes 3076
  21.2 115.8 %copy-start.104 = (f32[384]{0:T(512)}, f32[384]{0:T(512)S(1)}, u32[]{:S(2)}) copy-start(f32[384]{0:T(512)S(1)} %get-tuple-element.203) | copy-start | bytes 4612
  21.2 115.8 %copy-start.106 = (f32[384]{0:T(512)}, f32[384]{0:T(512)S(1)}, u32[]{:S(2)}) copy-start(f32[384]{0:T(512)S(1)} %get-tuple-element.204) | copy-start | bytes 4612
  21.2 115.8 %copy-start.108 = (f32[384]{0:T(512)}, f32[384]{0:T(512)S(1)}, u32[]{:S(2)}) copy-start(f32[384]{0:T(512)S(1)} %get-tuple-element.205) | copy-start | bytes 4612
  21.3 115.8 %copy-start.110 = (f32[384]{0:T(512)}, f32[384]{0:T(512)S(1)}, u32[]{:S(2)}) copy-start(f32[384]{0:T(512)S(1)} %get-tuple-element.206) | copy-start | bytes 4612
  21.5 112.9 %copy-start.151 = (f32[6]{0:T(128)}, f32[6]{0:T(128)S(1)}, u32[]{:S(2)}) copy-start(f32[6]{0:T(128)S(1)} %exponential_negate_fusion) | copy-start | bytes 76
  21.5 113.9 %copy-start.119 = (f32[1,256]{1,0:T(1,128)}, f32[1,256]{1,0:T(1,128)S(1)}, u32[]{:S(2)}) copy-start(f32[1,256]{1,0:T(1,128)S(1)} %get-tuple-element.272) | copy-start | bytes 3076
  21.5 113.9 %copy-start.121 = (f32[1,256]{1,0:T(1,128)}, f32[1,256]{1,0:T(1,128)S(1)}, u32[]{:S(2)}) copy-start(f32[1,256]{1,0:T(1,128)S(1)} %get-tuple-element.273) | copy-start | bytes 3076
  21.6 113.9 %copy-start.123 = (f32[1,256]{1,0:T(1,128)}, f32[1,256]{1,0:T(1,128)S(1)}, u32[]{:S(2)}) copy-start(f32[1,256]{1,0:T(1,128)S(1)} %get-tuple-element.275) | copy-start | bytes 3076
  21.6 113.9 %copy-start.125 = (f32[1,256]{1,0:T(1,128)}, f32[1,256]{1,0:T(1,128)S(1)}, u32[]{:S(2)}) copy-start(f32[1,256]{1,0:T(1,128)S(1)} %get-tuple-element.274) | copy-start | bytes 3076
  21.8 112.4 %copy-start.42 = (bf16[256,1024]{1,0:T(8,128)(2,1)}, bf16[256,1024]{1,0:T(8,128)(2,1)S(1)}, u32[]{:S(2)}) copy-start(bf16[256,1024]{1,0:T(8,128)(2,1)S(1)} %fusion.54) | copy-start | bytes 1572868
  21.8 119.6 %copy-start.139 = (f32[32]{0:T(128)}, f32[32]{0:T(128)S(1)}, u32[]{:S(2)}) copy-start(f32[32]{0:T(128)S(1)} %negate_power_fusion) | copy-start | bytes 388
  23.0 111.4 %copy-start.128 = (f32[6]{0:T(128)S(1)}, f32[6]{0:T(128)}, u32[]{:S(2)}) copy-start(f32[6]{0:T(128)} %param.32) | copy-start | bytes 76
  138.3 43.8 %copy-start.16 = (f32[256,384]{0,1:T(8,128)}, f32[256,384]{0,1:T(8,128)S(1)}, u32[]{:S(2)}) copy-start(f32[256,384]{0,1:T(8,128)S(1)} %copy.297) | copy-start | bytes 1179652
  139.5 99.6 %all-reduce.28.cloned.1.call-start = ((), (), s32[]{:S(2)}) async-start(), calls=%async_computation.4 | async-start | bytes 2097152 | tf_op jit(solution)/shard_map/psum | solution.py:160
  141.6 41.5 %copy-start.79 = (f32[256,32]{0,1:T(8,128)}, f32[256,32]{0,1:T(8,128)S(1)}, u32[]{:S(2)}) copy-start(f32[256,32]{0,1:T(8,128)S(1)} %get-tuple-element.276) | copy-start | bytes 98308
  141.6 41.5 %copy-start.81 = (f32[256,32]{0,1:T(8,128)}, f32[256,32]{0,1:T(8,128)S(1)}, u32[]{:S(2)}) copy-start(f32[256,32]{0,1:T(8,128)S(1)} %get-tuple-element.277) | copy-start | bytes 98308
  142.9 40.2 %copy-start.75 = (bf16[256,2,32]{0,2,1:T(8,128)(2,1)}, bf16[256,2,32]{0,2,1:T(8,128)(2,1)S(1)}, u32[]{:S(2)}) copy-start(bf16[256,2,32]{0,2,1:T(8,128)(2,1)S(1)} %get-tuple-element.252) | copy-start | bytes 98308
  144.0 50.0 %copy-start.85 = (f32[256,256]{1,0:T(8,128)}, f32[256,256]{1,0:T(8,128)S(1)}, u32[]{:S(2)}) copy-start(f32[256,256]{1,0:T(8,128)S(1)} %fusion.132) | copy-start | bytes 786436
  203.8 82.9 %all-reduce.30.cloned.1.call-start = ((), (), s32[]{:S(2)}) async-start(), calls=%async_computation.6 | async-start | bytes 2097152 | tf_op jit(solution)/shard_map/psum | solution.py:160
  249.8 126.0 %reduce-scatter.6.cloned.1.call-start = ((), (), s32[]{:S(2)}) async-start(), calls=%async_computation.7 | async-start | bytes 1474560 | tf_op jit(solution)/shard_map/reduce_scatter | solution.py:152
  310.0 157.3 %all-reduce.32.cloned.1.call-start = ((), (), s32[]{:S(2)}) async-start(), calls=%async_computation.8 | async-start | bytes 3244032 | tf_op jit(solution)/shard_map/psum | solution.py:160
  318.3 60.1 %copy-start.19 = (f32[256,384]{0,1:T(8,128)S(1)}, f32[256,384]{0,1:T(8,128)}, u32[]{:S(2)}) copy-start(f32[256,384]{0,1:T(8,128)} %copy-done.16) | copy-start | bytes 1179652
  323.2 60.3 %copy-start.96 = (f32[6,256]{1,0:T(8,128)S(1)}, f32[6,256]{1,0:T(8,128)}, u32[]{:S(2)}) copy-start(f32[6,256]{1,0:T(8,128)} %copy-done.94) | copy-start | bytes 18436
  323.2 60.4 %copy-start.129 = (f32[6]{0:T(128)S(1)}, f32[6]{0:T(128)}, u32[]{:S(2)}) copy-start(f32[6]{0:T(128)} %param.32) | copy-start | bytes 76
  323.2 60.4 %copy-start.142 = (f32[6]{0:T(128)S(1)}, f32[6]{0:T(128)}, u32[]{:S(2)}) copy-start(f32[6]{0:T(128)} %copy-done.141) | copy-start | bytes 76
  397.7 16.0 %collective-permute-start.1 = (f32[16,640]{1,0:T(8,128)}, f32[16,640]{1,0:T(8,128)}, u32[]{:S(2)}, u32[]{:S(2)}) collective-permute-start(f32[16,640]{1,0:T(8,128)} %pad_maximum_fusion.13), channel_id=1, source_target_pairs={{4,0},{8,4},{12,8},{16,12},{20,16},{24,20},{28,24},{5,1},{9,5},{13... | collective-permute-start | bytes 122888 | tf_op jit(solution)/shard_map/ppermute | solution.py:21
  422.0 73.3 %reduce-scatter.4.cloned.1.call-start = ((), (), s32[]{:S(2)}) async-start(), calls=%async_computation.5 | async-start | bytes 1310720 | tf_op jit(solution)/shard_map/reduce_scatter | solution.py:398
  429.9 202.5 %reduce-scatter.8.cloned.1.call-start = ((), (), s32[]{:S(2)}) async-start(), calls=%async_computation.9 | async-start | bytes 8257536 | tf_op jit(solution)/shard_map/reduce_scatter | solution.py:156
  (130 other events, 794.8 us)
Sparse Core Ops, SparseCore 0:
  16.3 114.8 all-gather.3
  139.6 40.2 all-gather.5
  203.9 35.0 all-reduce.27
  249.9 36.7 all-reduce.29
  310.1 65.6 reduce-scatter.5
  422.1 45.1 all-reduce.31
  470.5 24.7 reduce-scatter.3
  498.9 133.4 reduce-scatter.7
